TPU v7x, 32 devices: a whole 2x2x4 slice. The times are simulated.
32 devices in a mesh: tile: 16 (over z, x, core), wave: 2 (over y).
Axes of the slice: x: 2, y: 2, z: 4, core: 2. Of those that a mesh axis runs over, the one named last changes fastest.
Arguments:
- params: float32 [9, 256, 128], P(None, 'tile'), may hold values from -6 to 6
- dual_in: float32 [2, 9, 256, 128], P(None, None, 'tile'), may hold values from -4 to 4
- jacobian: bfloat16 [4, 9, 256, 128], P(None, None, 'tile'), may hold values from -3 to 3
- response: float32 [9, 64], P(None, 'wave'), may hold values from -5 to 5
- observed: bfloat16 [4, 64, 256, 128], P(None, 'wave', 'tile'), may hold values from -6 to 6
- psf: bfloat16 [17, 17], replicated, may hold values from -0.375 to 0.375
- step_size: float32 [], replicated, may hold values from 0.03 to 0.06
- dual_step: float32 [], replicated, may hold values from 0.5 to 1
- tv_bound: float32 [], replicated, may hold values from 1 to 2
- clip_bound: float32 [], replicated, may hold values from 0.5 to 1
Outputs:
- params_out: float32 [9, 256, 128], P(None, 'tile')
- dual_out: float32 [2, 9, 256, 128], P(None, None, 'tile')
- misfit: float32 [], replicated
All inputs are finite; a program needn't handle non-finite values.
Results may differ from a plain program's by a relative error of at most 0.0033.
Values may be sent and summed in bfloat16 or wider, within the bound.
A program may use at most 128 MiB of HBM per device.

v0:
```python
import jax
import jax.numpy as jnp
from jax import lax
from jax.sharding import PartitionSpec as P


def passed_along(x, axis, by):
    devices = lax.axis_size(axis)
    return lax.ppermute(x, axis, [(i, (i + by) % devices) for i in range(devices)])


def padded_2(block, sides, width):
    for axis, dim in sides:
        count = lax.axis_size(axis)
        forward = [(i, i + 1) for i in range(count - 1)]
        forward.append((count - 1, 0))
        backward = [(target, source) for source, target in forward]
        low = lax.ppermute(
            lax.slice_in_dim(block, block.shape[dim] - width, None, axis=dim), axis, forward
        )
        high = lax.ppermute(lax.slice_in_dim(block, 0, width, axis=dim), axis, backward)
        block = jnp.concatenate([low, block, high], axis=dim)
    return block


def toeplitz(psf, ncol):
    rows = jnp.arange(ncol, dtype=jnp.int32)[:, None]
    cols = jnp.arange(ncol, dtype=jnp.int32)[None, :]
    offset = (rows - cols + 8) % ncol
    onehot = (offset[None] == jnp.arange(17, dtype=jnp.int32)[:, None, None]).astype(jnp.float32)
    mats = jnp.einsum(
        "ab,bkj->akj", psf.astype(jnp.float32), onehot, precision=lax.Precision.HIGHEST
    )
    return mats.astype(jnp.bfloat16)


def blur_rows(padded, mats, adjoint):
    count = padded.shape[1] - 16
    total = jnp.zeros((padded.shape[0], count, padded.shape[2]), jnp.float32)
    for tap in range(17):
        window = padded[:, tap : tap + count]
        if adjoint:
            total = total + jnp.einsum(
                "nrk,jk->nrj", window, mats[16 - tap], preferred_element_type=jnp.float32
            )
        else:
            total = total + jnp.einsum(
                "nrk,kj->nrj", window, mats[tap], preferred_element_type=jnp.float32
            )
    return total


def synthesize(jac_band, state, response):
    terms = jac_band.astype(jnp.float32) * state[None]
    synthetic = jnp.einsum("pl,spij->slij", response, terms, precision=lax.Precision.HIGHEST)
    stokes, waves, rows, cols = synthetic.shape
    return synthetic.reshape(stokes * waves, rows, cols).astype(jnp.bfloat16)


def huber_total(resid, clip_bound):
    size = jnp.abs(resid)
    return jnp.sum(
        jnp.where(
            size <= clip_bound,
            0.5 * resid * resid,
            clip_bound * size - 0.5 * clip_bound * clip_bound,
        )
    )


def per_device(
    params, dual_in, jacobian, response, observed, psf, step_size, dual_step, tv_bound, clip_bound
):
    stokes, waves, rows, ncol = observed.shape
    images = stokes * waves
    mats = toeplitz(psf, ncol)
    flat_obs = observed.reshape(images, rows, ncol)
    following = passed_along(params[:, :1], "tile", -1)
    grad_r = jnp.concatenate([params[:, 1:], following], axis=1) - params
    grad_c = jnp.roll(params, -1, axis=2) - params
    dual_out = jnp.clip(dual_in + dual_step * jnp.stack([grad_r, grad_c]), -tv_bound, tv_bound)
    preceding = passed_along(dual_out[0][:, -1:], "tile", 1)
    divergence = dual_out[0] - jnp.concatenate([preceding, dual_out[0][:, :-1]], axis=1)
    divergence = divergence + (dual_out[1] - jnp.roll(dual_out[1], 1, axis=2))
    state = params
    misfit = jnp.float32(0.0)
    for step in range(2):
        synthetic = synthesize(jacobian, state, response)
        padded = padded_2(synthetic, (("tile", 1),), 8)
        blurred = blur_rows(padded, mats, False)
        resid = blurred - flat_obs.astype(jnp.float32)
        huber = huber_total(resid, clip_bound)
        weighted = jnp.clip(resid, -clip_bound, clip_bound).astype(jnp.bfloat16)
        padded_back = padded_2(weighted, (("tile", 1),), 8)
        back = blur_rows(padded_back, mats, True)
        along = jnp.einsum(
            "pl,slij->spij",
            response,
            back.reshape(stokes, waves, rows, ncol),
            precision=lax.Precision.HIGHEST,
        )
        partial_grad, huber = (jnp.sum(jacobian.astype(jnp.float32) * along, axis=0), huber)
        if step == 0:
            total_count = images * lax.axis_size("wave") * rows * lax.axis_size("tile") * ncol
            misfit = lax.psum(huber, ("tile", "wave")) / total_count
        share = rows // lax.axis_size("wave")
        start = lax.axis_index("wave") * share
        grad_share = lax.psum_scatter(partial_grad, "wave", scatter_dimension=1, tiled=True)
        state_share = lax.dynamic_slice_in_dim(state, start, share, 1)
        div_share = lax.dynamic_slice_in_dim(divergence, start, share, 1)
        state_share = state_share - step_size * (grad_share - div_share)
        state = lax.all_gather(state_share, "wave", axis=1, tiled=True)
    return (state, dual_out, misfit)


def solution(mesh):
    in_specs = (
        P(None, "tile", None),
        P(None, None, "tile", None),
        P(None, None, "tile", None),
        P(None, "wave"),
        P(None, "wave", "tile", None),
        P(),
        P(),
        P(),
        P(),
        P(),
    )
    out_specs = (P(None, "tile", None), P(None, None, "tile", None), P())
    return jax.shard_map(
        per_device, mesh=mesh, in_specs=in_specs, out_specs=out_specs, check_vma=False
    )
```

profile of v0, /device:TPU:0, one launch (start us, length us, event | category | flops | bytes accessed | tf_op | source)
XLA Modules:
  0.0 170.7 jit_solution(4599097316442798490)
XLA Ops:
  7.2 0.9 copy.64
  8.2 1.9 %fusion.64 = bf16[4,32,16,128]{3,1,2,0:T(8,128)(2,1)S(1)} fusion(bf16[4,9,16,128]{3,2,1,0:T(8,128)(2,1)} %param.12, f32[9,16,128]{2,0,1:T(8,128)S(1)} %copy.64, f32[9,32]{1,0:T(8,128)S(1)} %copy-done), kind=kOutput, calls=%fused_computation.76 | convolution fusion | flops 28721152 | bytes 746624 | tf_op jit(solution)/shard_map/pl,spij->slij/dot_general | solution.py:55
  10.4 0.8 copy.138
  11.6 0.8 copy.137
  12.4 5.0 %collective-permute-start.1 = (bf16[128,8,128]{2,0,1:T(8,128)(2,1)}, bf16[128,8,128]{2,0,1:T(8,128)(2,1)}, u32[]{:S(2)}, u32[]{:S(2)}) collective-permute-start(bf16[128,8,128]{2,0,1:T(8,128)(2,1)} %copy.137), channel_id=1, source_target_pairs={{2,0},{4,2},{6,4},{8,6},{10,8},{12,10},{14,12},{16,14},{18,16},{20... | collective-permute-start | bytes 786440 | tf_op jit(solution)/shard_map/ppermute | solution.py:21
  17.3 0.7 collective-permute-start.4
  18.5 1.1 fusion.227
  20.3 0.6 copy.102
  20.9 0.6 copy.101
  21.5 0.6 copy.100
  22.1 0.6 copy.99
  22.7 0.6 copy.98
  23.4 0.6 copy.97
  24.0 0.6 copy.96
  24.6 0.6 copy.95
  25.2 0.6 copy.109
  25.8 0.6 copy.108
  26.5 0.6 copy.107
  27.1 0.6 copy.106
  27.7 0.6 copy.105
  28.3 0.6 copy.110
  28.9 0.6 copy.111
  29.6 0.6 copy.104
  32.9 1.0 fusion.83
  33.9 1.0 fusion.80
  35.2 1.0 constant_dynamic-update-slice_fusion.1
  41.3 1.0 constant_dynamic-update-slice_fusion.2
  47.1 0.6 fusion.61
  47.9 0.6 minimum_convert_fusion
  48.7 4.7 %collective-permute-start.3 = (bf16[128,8,128]{2,0,1:T(8,128)(2,1)S(1)}, bf16[128,8,128]{2,0,1:T(8,128)(2,1)S(1)}, u32[]{:S(2)}, u32[]{:S(2)}) collective-permute-start(bf16[128,8,128]{2,0,1:T(8,128)(2,1)S(1)} %get-tuple-element.35), channel_id=1, source_target_pairs={{2,0},{4,2},{6,4},{8,6},{10,8},{12,10},{14,12},{16,14},{18,16},{20... | collective-permute-start | bytes 786440 | tf_op jit(solution)/shard_map/ppermute | solution.py:21
  53.6 3.6 %collective-permute-done.2 = bf16[128,8,128]{2,0,1:T(8,128)(2,1)S(1)} collective-permute-done((bf16[128,8,128]{2,0,1:T(8,128)(2,1)S(1)}, bf16[128,8,128]{2,0,1:T(8,128)(2,1)S(1)}, u32[]{:S(2)}, u32[]{:S(2)}) %collective-permute-start.2) | collective-permute-done | bytes 262176 | tf_op jit(solution)/shard_map/ppermute | solution.py:18
  63.0 1.3 fusion.68
  64.6 9.5 %reduce-scatter.3.cloned.1.call-done = f32[9,8,128]{2,0,1:T(8,128)} async-done(((f32[9,16,128]{2,0,1:T(8,128)}), f32[9,8,128]{2,0,1:T(8,128)}) %reduce-scatter.3.cloned.1.call-update) | async-done | bytes 36880 | tf_op jit(solution)/shard_map/reduce_scatter | solution.py:108
  74.1 0.9 multiply_subtract_fusion.1
  75.1 4.6 %all_gather.6 = f32[9,16,128]{2,1,0:T(8,128)S(1)} all-gather(f32[9,8,128]{2,1,0:T(8,128)S(1)} %copy.82), channel_id=1, replica_groups=mesh['tile'=16,'wave'=2] {'wave'}, dimensions={1}, use_global_device_ids=true | all-gather | bytes 110592 | tf_op jit(solution)/shard_map/all_gather | solution.py:112
  79.7 1.0 fusion.65
  81.2 4.5 %collective-permute-start.7 = (bf16[128,8,128]{2,0,1:T(8,128)(2,1)S(1)}, bf16[128,8,128]{2,0,1:T(8,128)(2,1)S(1)}, u32[]{:S(2)}, u32[]{:S(2)}) collective-permute-start(bf16[128,8,128]{2,0,1:T(8,128)(2,1)S(1)} %copy.139), channel_id=1, source_target_pairs={{2,0},{4,2},{6,4},{8,6},{10,8},{12,10},{14,12},{16,14},{18,16},{20... | collective-permute-start | bytes 786440 | tf_op jit(solution)/shard_map/ppermute | solution.py:21
  86.0 3.8 %collective-permute-done.6 = bf16[128,8,128]{2,0,1:T(8,128)(2,1)S(1)} collective-permute-done((bf16[128,8,128]{2,0,1:T(8,128)(2,1)S(1)}, bf16[128,8,128]{2,0,1:T(8,128)(2,1)S(1)}, u32[]{:S(2)}, u32[]{:S(2)}) %collective-permute-start.6) | collective-permute-done | bytes 262176 | tf_op jit(solution)/shard_map/ppermute | solution.py:18
  100.9 0.6 fusion.62
  101.6 4.4 %collective-permute-start.9 = (bf16[128,8,128]{2,0,1:T(8,128)(2,1)S(1)}, bf16[128,8,128]{2,0,1:T(8,128)(2,1)S(1)}, u32[]{:S(2)}, u32[]{:S(2)}) collective-permute-start(bf16[128,8,128]{2,0,1:T(8,128)(2,1)S(1)} %get-tuple-element.29), channel_id=1, source_target_pairs={{2,0},{4,2},{6,4},{8,6},{10,8},{12,10},{14,12},{16,14},{18,16},{20... | collective-permute-start | bytes 786440 | tf_op jit(solution)/shard_map/ppermute | solution.py:21
  106.4 3.8 %collective-permute-done.8 = bf16[128,8,128]{2,0,1:T(8,128)(2,1)S(1)} collective-permute-done((bf16[128,8,128]{2,0,1:T(8,128)(2,1)S(1)}, bf16[128,8,128]{2,0,1:T(8,128)(2,1)S(1)}, u32[]{:S(2)}, u32[]{:S(2)}) %collective-permute-start.8) | collective-permute-done | bytes 262176 | tf_op jit(solution)/shard_map/ppermute | solution.py:18
  115.5 1.4 fusion.69
  116.9 0.9 fusion.71
  117.8 0.7 copy.93
  118.5 37.0 %psum.7 = f32[]{:T(128)} all-reduce(f32[]{:T(128)} %fusion.71), channel_id=1, replica_groups=mesh['tile'=16,'wave'=2] {'tile','wave'}, use_global_device_ids=true, to_apply=%region_5.6 | all-reduce | flops 1 | bytes 8 | tf_op jit(solution)/shard_map/psum | solution.py:105
  156.2 0.9 multiply_subtract_fusion
  157.1 5.1 %all_gather.7 = f32[9,16,128]{2,1,0:T(8,128)S(1)} all-gather(f32[9,8,128]{2,1,0:T(8,128)S(1)} %copy.92), channel_id=1, replica_groups=mesh['tile'=16,'wave'=2] {'wave'}, dimensions={1}, use_global_device_ids=true | all-gather | bytes 110592 | tf_op jit(solution)/shard_map/all_gather | solution.py:112
  162.1 0.6 copy.150
  (193 shorter events, 36.0 us)
Async XLA Ops:
  7.2 1.0 copy-start
  7.2 66.9 %reduce-scatter.3.cloned.1.call-start = ((), (), s32[]{:S(2)}) async-start(), calls=%async_computation.2 | async-start | bytes 196608 | tf_op jit(solution)/shard_map/reduce_scatter | solution.py:108
  10.3 7.7 %copy-start.41 = (bf16[17,17]{1,0:T(8,128)(2,1)S(1)}, bf16[17,17]{1,0:T(8,128)(2,1)}, u32[]{:S(2)}) copy-start(bf16[17,17]{1,0:T(8,128)(2,1)} %param.15) | copy-start | bytes 1738
  11.1 24.1 %collective-permute-start = (bf16[128,8,128]{2,0,1:T(8,128)(2,1)}, bf16[128,8,128]{2,0,1:T(8,128)(2,1)}, u32[]{:S(2)}, u32[]{:S(2)}) collective-permute-start(bf16[128,8,128]{2,0,1:T(8,128)(2,1)} %copy.138), channel_id=1, source_target_pairs={{0,2},{2,4},{4,6},{6,8},{8,10},{10,12},{12,14},{14,16},{16,18},{18... | collective-permute-start | bytes 786440 | tf_op jit(solution)/shard_map/ppermute | solution.py:18
  12.4 28.9 %collective-permute-start.1 = (bf16[128,8,128]{2,0,1:T(8,128)(2,1)}, bf16[128,8,128]{2,0,1:T(8,128)(2,1)}, u32[]{:S(2)}, u32[]{:S(2)}) collective-permute-start(bf16[128,8,128]{2,0,1:T(8,128)(2,1)} %copy.137), channel_id=1, source_target_pairs={{2,0},{4,2},{6,4},{8,6},{10,8},{12,10},{14,12},{16,14},{18,16},{20... | collective-permute-start | bytes 786440 | tf_op jit(solution)/shard_map/ppermute | solution.py:21
  17.3 15.6 %collective-permute-start.4 = (f32[9,1,128]{2,0,1:T(8,128)S(1)}, f32[9,1,128]{2,0,1:T(8,128)S(1)}, u32[]{:S(2)}, u32[]{:S(2)}) collective-permute-start(f32[9,1,128]{2,0,1:T(8,128)S(1)} %slice.540), channel_id=1, source_target_pairs={{0,30},{2,0},{4,2},{6,4},{8,6},{10,8},{12,10},{14,12},{16,14},{18,... | collective-permute-start | bytes 13832 | tf_op jit(solution)/shard_map/ppermute | solution.py:9
  20.0 10.9 %copy-start.40 = (bf16[4,32,16,128]{3,2,1,0:T(8,128)(2,1)S(1)}, bf16[4,32,16,128]{3,2,1,0:T(8,128)(2,1)}, u32[]{:S(2)}) copy-start(bf16[4,32,16,128]{3,2,1,0:T(8,128)(2,1)} %param.14) | copy-start | bytes 1572868
  35.0 1.5 copy-start.2
  35.0 1.5 copy-start.38
  35.1 1.3 copy-start.8
  35.1 29.4 %collective-permute-start.5 = (f32[9,1,128]{2,0,1:T(8,128)S(1)}, f32[9,1,128]{2,0,1:T(8,128)S(1)}, u32[]{:S(2)}, u32[]{:S(2)}) collective-permute-start(f32[9,1,128]{2,0,1:T(8,128)S(1)} %slice.544), channel_id=1, source_target_pairs={{0,2},{2,4},{4,6},{6,8},{8,10},{10,12},{12,14},{14,16},{16,18},{18... | collective-permute-start | bytes 13832 | tf_op jit(solution)/shard_map/ppermute | solution.py:9
  36.4 0.8 copy-start.10
  37.2 0.8 copy-start.12
  38.0 0.8 copy-start.14
  38.7 0.8 copy-start.16
  39.5 0.8 copy-start.18
  40.2 0.8 copy-start.20
  41.0 1.3 copy-start.24
  41.3 1.3 copy-start.26
  42.6 0.8 copy-start.28
  43.3 0.8 copy-start.30
  44.1 0.8 copy-start.32
  44.9 0.8 copy-start.34
  45.6 0.8 copy-start.22
  46.4 0.8 copy-start.4
  47.1 0.8 copy-start.6
  48.5 4.8 %copy-start.37 = (bf16[1,128,128]{2,1,0:T(8,128)(2,1)S(1)}, bf16[1,128,128]{2,1,0:T(8,128)(2,1)}, u32[]{:S(2)}) copy-start(bf16[1,128,128]{2,1,0:T(8,128)(2,1)} %copy-done.36) | copy-start | bytes 98308
  48.6 8.6 %collective-permute-start.2 = (bf16[128,8,128]{2,0,1:T(8,128)(2,1)S(1)}, bf16[128,8,128]{2,0,1:T(8,128)(2,1)S(1)}, u32[]{:S(2)}, u32[]{:S(2)}) collective-permute-start(bf16[128,8,128]{2,0,1:T(8,128)(2,1)S(1)} %get-tuple-element.34), channel_id=1, source_target_pairs={{0,2},{2,4},{4,6},{6,8},{8,10},{10,12},{12,14},{14,16},{16,18},{18... | collective-permute-start | bytes 786440 | tf_op jit(solution)/shard_map/ppermute | solution.py:18
  48.7 10.7 %collective-permute-start.3 = (bf16[128,8,128]{2,0,1:T(8,128)(2,1)S(1)}, bf16[128,8,128]{2,0,1:T(8,128)(2,1)S(1)}, u32[]{:S(2)}, u32[]{:S(2)}) collective-permute-start(bf16[128,8,128]{2,0,1:T(8,128)(2,1)S(1)} %get-tuple-element.35), channel_id=1, source_target_pairs={{2,0},{4,2},{6,4},{8,6},{10,8},{12,10},{14,12},{16,14},{18,16},{20... | collective-permute-start | bytes 786440 | tf_op jit(solution)/shard_map/ppermute | solution.py:21
  62.0 0.9 copy-start.1
  63.0 11.1 %copy-start.3 = (f32[9,16,128]{2,0,1:T(8,128)S(1)}, f32[9,16,128]{2,0,1:T(8,128)}, u32[]{:S(2)}) copy-start(f32[9,16,128]{2,0,1:T(8,128)} %copy-done.2) | copy-start | bytes 221188
  63.0 11.1 %copy-start.39 = (f32[9,16,128]{2,0,1:T(8,128)S(1)}, f32[9,16,128]{2,0,1:T(8,128)}, u32[]{:S(2)}) copy-start(f32[9,16,128]{2,0,1:T(8,128)} %copy-done.38) | copy-start | bytes 221188
  64.3 91.8 %reduce-scatter.5.cloned.1.call-start = ((), (), s32[]{:S(2)}) async-start(), calls=%async_computation.3 | async-start | bytes 196608 | tf_op jit(solution)/shard_map/reduce_scatter | solution.py:108
  81.1 8.6 %collective-permute-start.6 = (bf16[128,8,128]{2,0,1:T(8,128)(2,1)S(1)}, bf16[128,8,128]{2,0,1:T(8,128)(2,1)S(1)}, u32[]{:S(2)}, u32[]{:S(2)}) collective-permute-start(bf16[128,8,128]{2,0,1:T(8,128)(2,1)S(1)} %copy.140), channel_id=1, source_target_pairs={{0,2},{2,4},{4,6},{6,8},{8,10},{10,12},{12,14},{14,16},{16,18},{18... | collective-permute-start | bytes 786440 | tf_op jit(solution)/shard_map/ppermute | solution.py:18
  81.2 13.6 %collective-permute-start.7 = (bf16[128,8,128]{2,0,1:T(8,128)(2,1)S(1)}, bf16[128,8,128]{2,0,1:T(8,128)(2,1)S(1)}, u32[]{:S(2)}, u32[]{:S(2)}) collective-permute-start(bf16[128,8,128]{2,0,1:T(8,128)(2,1)S(1)} %copy.139), channel_id=1, source_target_pairs={{2,0},{4,2},{6,4},{8,6},{10,8},{12,10},{14,12},{16,14},{18,16},{20... | collective-permute-start | bytes 786440 | tf_op jit(solution)/shard_map/ppermute | solution.py:21
  85.9 4.0 %copy-start.9 = (bf16[1,128,128]{2,1,0:T(8,128)(2,1)S(1)}, bf16[1,128,128]{2,1,0:T(8,128)(2,1)}, u32[]{:S(2)}) copy-start(bf16[1,128,128]{2,1,0:T(8,128)(2,1)} %copy.102) | copy-start | bytes 98308
  90.0 0.8 copy-start.11
  90.7 0.8 copy-start.13
  91.5 0.8 copy-start.15
  92.3 0.8 copy-start.17
  93.0 0.8 copy-start.19
  93.8 0.8 copy-start.21
  94.5 0.8 copy-start.25
  94.8 0.8 copy-start.27
  95.6 0.8 copy-start.29
  96.3 0.8 copy-start.31
  101.6 8.5 %collective-permute-start.8 = (bf16[128,8,128]{2,0,1:T(8,128)(2,1)S(1)}, bf16[128,8,128]{2,0,1:T(8,128)(2,1)S(1)}, u32[]{:S(2)}, u32[]{:S(2)}) collective-permute-start(bf16[128,8,128]{2,0,1:T(8,128)(2,1)S(1)} %get-tuple-element.28), channel_id=1, source_target_pairs={{0,2},{2,4},{4,6},{6,8},{8,10},{10,12},{12,14},{14,16},{16,18},{18... | collective-permute-start | bytes 786440 | tf_op jit(solution)/shard_map/ppermute | solution.py:18
  101.6 10.6 %collective-permute-start.9 = (bf16[128,8,128]{2,0,1:T(8,128)(2,1)S(1)}, bf16[128,8,128]{2,0,1:T(8,128)(2,1)S(1)}, u32[]{:S(2)}, u32[]{:S(2)}) collective-permute-start(bf16[128,8,128]{2,0,1:T(8,128)(2,1)S(1)} %get-tuple-element.29), channel_id=1, source_target_pairs={{2,0},{4,2},{6,4},{8,6},{10,8},{12,10},{14,12},{16,14},{18,16},{20... | collective-permute-start | bytes 786440 | tf_op jit(solution)/shard_map/ppermute | solution.py:21
  (6 other events, 4.4 us)
Sparse Core Ops, SparseCore 0:
  64.4 9.5 reduce-scatter.2
  117.0 8.7 reduce-scatter.4
where the time goes:
time: 173 us; the launch traced here: 171 us
  blocking collectives  46.7 us (27%)
  local copies, waits for them, and re-layouts  31.2 us (18%)
  matrix products  28 us (16%)
  waiting for transfers between devices  20.7 us (12%)
  starting transfers between devices  20 us (12%)
  between operations  19.2 us (11%)
  other arithmetic  4.92 us (3%)
    psum x1, blocking collectives, per_device(): misfit = lax.psum(huber, ('tile', 'wave')) / total_count  37 us
    unnamed x110, local copies, waits for them, and re-layouts  27.6 us
    ppermute x4, starting transfers between devices, padded_2(): lax.ppermute(lax.slice_in_dim(block, 0, width, axis=dim), axis, backward)  18.5 us
    dot_general x34, matrix products, blur_rows(): jnp.einsum('nrk,jk->nrj', window, mats[16 - tap], preferred_element_type=...  11.2 us
    ppermute x4, waiting for transfers between devices, padded_2(): lax.ppermute(lax.slice_in_dim(block, block.shape[dim] - width, None, axis...  11.1 us
    dot_general x34, matrix products, blur_rows(): jnp.einsum('nrk,kj->nrj', window, mats[tap], preferred_element_type=jnp.f...  10.7 us
    all_gather x2, blocking collectives, per_device(): state = lax.all_gather(state_share, 'wave', axis=1, tiled=True)  9.68 us
    reduce_scatter x2, waiting for transfers between devices, per_device(): lax.psum_scatter(partial_grad, 'wave', scatter_dimension=1, tiled=True)  9.54 us
  transfers between devices with their start and end apart: 12, of which 4 were waited for; matrix products, arithmetic and copies ran while one was open for 21% of the time, Pallas kernels for 0%

commit v1 on v0

v1 whole, which is shorter than its diff:
```python
import functools

import jax
import jax.numpy as jnp
from jax import lax
from jax.experimental import pallas as pl
from jax.experimental.pallas import tpu as pltpu
from jax.sharding import PartitionSpec as P

MESH = pl.DeviceIdType.MESH
HALO = 8
EDGE = 2 * HALO
TAPS = 17
PAIRS = 9
F32 = jnp.float32
BF16 = jnp.bfloat16


def split_hi_lo(value):
    high = value.astype(BF16).astype(F32)
    return high, value - high


def group_size(count):
    size = 1
    while size * size < count:
        size *= 2
    return size if count % size == 0 else count


def kernel(
    tiles, waves, total_count,
    params, dual, jac, obs, response, prow, step_size, dual_step, tv_bound, clip_bound,
    x_out, d_out, m_out,
    mats, obs_f, jac_f, terms, pairs, proj, acc, xpad, dpad, div, respad, rt, rbf, rtb,
    jac_up, jac_dn, par_up, par_dn, dual_up,
    contrib, wave_in, summed, edge_up, edge_dn,
    m_own, m_wave, m_group, m_cross,
    in_send, in_recv, w_send, w_recv, e_send, e_recv, mw_send, mw_recv,
    mg_send, mg_recv, mc_send, mc_recv,
):
    npar, rows, ncol = params.shape
    images = jac.shape[0]
    stokes = images // npar
    nwave = response.shape[1]
    nimg = stokes * nwave
    width = -(-images // 8) * 8
    padded = rows + EDGE
    npair = padded // 2
    opair = rows // 2
    me_t = lax.axis_index("tile")
    me_w = lax.axis_index("wave")
    up = lax.rem(me_t + tiles - 1, tiles)
    down = lax.rem(me_t + 1, tiles)
    gsize = group_size(tiles)
    ngroup = tiles // gsize
    my_group = me_t // gsize
    my_place = lax.rem(me_t, gsize)
    group_peers = [my_group * gsize + lax.rem(my_place + d, gsize) for d in range(1, gsize)]
    cross_peers = [lax.rem(my_group + d, ngroup) * gsize + my_place for d in range(1, ngroup)]
    wave_peers = [lax.rem(me_w + d, waves) for d in range(1, waves)]

    barrier = pltpu.get_barrier_semaphore()
    peers = [(t, me_w) for t in [up, down] + group_peers + cross_peers]
    peers += [(me_t, w) for w in wave_peers]
    for peer in peers:
        pl.semaphore_signal(barrier, inc=1, device_id=peer, device_id_type=MESH)
    pl.semaphore_wait(barrier, len(peers))

    def remote(src, dst, send, recv, peer):
        return pltpu.make_async_remote_copy(
            src_ref=src, dst_ref=dst, send_sem=send, recv_sem=recv,
            device_id=peer, device_id_type=MESH,
        )

    first = [
        remote(params.at[:, pl.ds(rows - HALO, HALO)], par_up, in_send.at[0], in_recv.at[0], (down, me_w)),
        remote(params.at[:, pl.ds(0, HALO)], par_dn, in_send.at[1], in_recv.at[1], (up, me_w)),
        remote(dual.at[0, :, pl.ds(rows - HALO, HALO)], dual_up, in_send.at[2], in_recv.at[2], (down, me_w)),
        remote(jac.at[:, pl.ds(rows - EDGE, EDGE)], jac_up, in_send.at[3], in_recv.at[3], (down, me_w)),
        remote(jac.at[:, pl.ds(0, EDGE)], jac_dn, in_send.at[4], in_recv.at[4], (up, me_w)),
    ]
    for copy in first:
        copy.start()

    step = step_size[0]
    clip = clip_bound[0]
    bound = tv_bound[0]
    dstep = dual_step[0]

    zero_block = jnp.zeros((ncol, ncol), BF16)
    mats[0, 0:ncol, ncol:] = zero_block
    mats[PAIRS - 1, ncol:, 0:ncol] = zero_block
    for tap in range(TAPS):
        base = jnp.broadcast_to(prow[tap:tap + 1, :], (ncol, ncol))
        block = pltpu.roll(base, 0, 1, stride=1, stride_axis=0).astype(BF16)
        if tap % 2 == 0:
            mats[tap // 2, 0:ncol, 0:ncol] = block
            mats[tap // 2, ncol:, ncol:] = block
        else:
            mats[tap // 2, ncol:, 0:ncol] = block
            mats[tap // 2 + 1, 0:ncol, ncol:] = block

    respad[...] = jnp.zeros_like(respad)
    respad[0:npar, 0:nwave] = response[...]
    rt[...] = jnp.zeros_like(rt)
    spread = respad[...]
    for s in range(stokes):
        shifted = spread if s == 0 else pltpu.roll(spread, s * nwave, 1)
        for part in range(3):
            at = part * width + s * npar
            rt[at:at + npar, :] = shifted[0:npar]
    full = rt[...]
    high, low = split_hi_lo(full)
    place = lax.broadcasted_iota(jnp.int32, full.shape, 0)
    rbf[...] = jnp.where(place < 2 * width, high, low).T.astype(BF16)
    rtb[...] = jnp.concatenate([high[0:width], low[0:width]], axis=0).astype(BF16)

    obs_f[...] = obs[...].astype(F32).reshape(nimg * rows, ncol)
    for m in range(images):
        jac_f[m, HALO:HALO + rows, :] = jac[m].astype(F32)
    for m in range(images, width):
        terms[m * padded:(m + 1) * padded, :] = jnp.zeros((padded, ncol), F32)
    d1 = params[...]
    d1 = pltpu.roll(d1, ncol - 1, 2) - d1
    d1 = jnp.clip(dual[1] + dstep * d1, -bound, bound)
    d_out[1] = d1
    xpad[:, HALO:HALO + rows, :] = params[...]

    for copy in first:
        copy.wait()
    xpad[:, 0:HALO, :] = par_up[...]
    xpad[:, HALO + rows:, :] = par_dn[...]
    for m in range(images):
        jac_f[m, 0:HALO, :] = jac_up[m].astype(F32)[HALO:]
        jac_f[m, HALO + rows:, :] = jac_dn[m].astype(F32)[:HALO]
    d0 = xpad[:, HALO + 1:HALO + 1 + rows, :] - xpad[:, HALO:HALO + rows, :]
    d0 = jnp.clip(dual[0] + dstep * d0, -bound, bound)
    d_out[0] = d0
    edge = xpad[:, 1:HALO + 1, :] - xpad[:, 0:HALO, :]
    dpad[:, 0:HALO, :] = jnp.clip(dual_up[...] + dstep * edge, -bound, bound)
    dpad[:, HALO:, :] = d0
    div[...] = (d0 - dpad[:, HALO - 1:HALO - 1 + rows, :]) + (d1 - pltpu.roll(d1, 1, 2))

    zero_k = jnp.zeros((rbf.shape[1] - 3 * width, 2 * ncol), F32)
    own_first = me_w == 0

    for it in range(2):
        for m in range(images):
            terms[m * padded:(m + 1) * padded, :] = jac_f[m] * xpad[m % npar]
        for q in range(npair):
            for i in range(2):
                value = terms[pl.ds(2 * q + i, width, stride=padded), :]
                value = jnp.concatenate(split_hi_lo(value), axis=0).astype(BF16)
                pairs[q * 2 * width:(q + 1) * 2 * width, i * ncol:(i + 1) * ncol] = value
        total = None
        for k in range(PAIRS):
            window = pairs[k * 2 * width:(k + opair) * 2 * width, :]
            part = jnp.dot(window, mats[k], preferred_element_type=F32)
            total = part if total is None else total + part
        loss = jnp.zeros((8, ncol), F32)
        for r in range(opair):
            both = total[r * 2 * width:(r + 1) * 2 * width]
            bhi, blo = split_hi_lo(both[:width] + both[width:])
            stack = jnp.concatenate([bhi, blo, bhi, zero_k], axis=0).astype(BF16)
            blurred = jnp.dot(rbf[...], stack, preferred_element_type=F32)
            halves = []
            for i in range(2):
                target = obs_f[pl.ds(2 * r + i, nimg, stride=rows), :]
                resid = blurred[:, i * ncol:(i + 1) * ncol] - target
                held = jnp.clip(resid, -clip, clip)
                if it == 0:
                    huber = held * (resid - 0.5 * held)
                    loss = loss + jnp.sum(huber.reshape(nimg // 8, 8, ncol), axis=0)
                halves.append(held.astype(BF16))
            weighted = jnp.concatenate(halves, axis=1)
            both = jnp.dot(rtb[...], weighted, preferred_element_type=F32)
            value = jnp.concatenate(split_hi_lo(both[:width] + both[width:]), axis=0)
            proj[r * 2 * width:(r + 1) * 2 * width, :] = value.astype(BF16)
        copies_m = []
        if it == 0:
            m_own[...] = loss
            m_wave[me_w] = loss
            for d, w in enumerate(wave_peers):
                copies_m.append(remote(m_own, m_wave.at[me_w], mw_send.at[d], mw_recv.at[d], (me_t, w)))
            for copy in copies_m:
                copy.start()
        for k in range(PAIRS):
            back = lax.dot_general(
                proj[...], mats[k], (((1,), (1,)), ((), ())), preferred_element_type=F32
            )
            for q in range(opair):
                both = back[q * 2 * width:(q + 1) * 2 * width]
                both = both[:width] + both[width:]
                at = (k + q) * width
                if k == 0 or q == opair - 1:
                    acc[at:at + width, :] = both
                else:
                    acc[at:at + width, :] += both
        for q in range(npair):
            for i in range(2):
                value = acc[q * width:(q + 1) * width, i * ncol:(i + 1) * ncol]
                terms[pl.ds(2 * q + i, width, stride=padded), :] = value
        for p in range(npar):
            grad = None
            for s in range(stokes):
                m = s * npar + p
                part = jac_f[m] * terms[m * padded:(m + 1) * padded, :]
                grad = part if grad is None else grad + part
            grad = grad * (-step)
            centre = xpad[p, HALO:HALO + rows, :] + step * div[p]
            centre = jnp.where(own_first, centre, jnp.zeros_like(centre))
            value = jnp.concatenate(
                [grad[:HALO], grad[HALO:HALO + rows] + centre, grad[HALO + rows:]], axis=0
            )
            contrib[it, p] = value
            wave_in[it, me_w, p] = value
        copies_w = [
            remote(contrib.at[it], wave_in.at[it, me_w], w_send.at[it, d], w_recv.at[it, d], (me_t, w))
            for d, w in enumerate(wave_peers)
        ]
        for copy in copies_w:
            copy.start()
        if it == 1:
            mid = m_group[0]
            for g in range(1, gsize):
                mid = mid + m_group[g]
            m_own[...] = mid
            m_cross[my_group] = mid
            copies_c = [
                remote(m_own, m_cross.at[my_group], mc_send.at[d], mc_recv.at[d], (t, me_w))
                for d, t in enumerate(cross_peers)
            ]
            for copy in copies_c:
                copy.start()
        for copy in copies_w + copies_m:
            copy.wait()
        whole = wave_in[it, 0]
        for w in range(1, waves):
            whole = whole + wave_in[it, w]
        summed[it] = whole
        reach = EDGE if it == 0 else HALO
        copies_e = [
            remote(summed.at[it, :, pl.ds(0, reach)], edge_dn.at[it, :, pl.ds(0, reach)],
                   e_send.at[it, 0], e_recv.at[it, 0], (up, me_w)),
            remote(summed.at[it, :, pl.ds(padded - reach, reach)], edge_up.at[it, :, pl.ds(0, reach)],
                   e_send.at[it, 1], e_recv.at[it, 1], (down, me_w)),
        ]
        for copy in copies_e:
            copy.start()
        if it == 0:
            mid = m_wave[0]
            for w in range(1, waves):
                mid = mid + m_wave[w]
            m_own[...] = mid
            m_group[my_place] = mid
            copies_g = [
                remote(m_own, m_group.at[my_place], mg_send.at[d], mg_recv.at[d], (t, me_w))
                for d, t in enumerate(group_peers)
            ]
            for copy in copies_g:
                copy.start()
            for copy in copies_e + copies_g:
                copy.wait()
            xpad[:, 0:EDGE, :] = summed[0, :, 0:EDGE, :] + edge_up[0]
            if rows > EDGE:
                xpad[:, EDGE:rows, :] = summed[0, :, EDGE:rows, :]
            xpad[:, rows:, :] = summed[0, :, rows:, :] + edge_dn[0]
        else:
            for copy in copies_e + copies_c:
                copy.wait()
            x_out[:, 0:HALO, :] = summed[1, :, HALO:EDGE, :] + edge_up[1, :, 0:HALO, :]
            if rows > EDGE:
                x_out[:, HALO:rows - HALO, :] = summed[1, :, EDGE:rows, :]
            x_out[:, rows - HALO:, :] = summed[1, :, rows:rows + HALO, :] + edge_dn[1, :, 0:HALO, :]
            tot = m_cross[0]
            for g in range(1, ngroup):
                tot = tot + m_cross[g]
            m_out[0] = jnp.sum(tot) / total_count


def per_device(
    params, dual_in, jacobian, response, observed, psf, step_size, dual_step, tv_bound, clip_bound
):
    stokes, nwave, rows, ncol = observed.shape
    npar = params.shape[0]
    nimg = stokes * nwave
    images = stokes * npar
    width = -(-images // 8) * 8
    kdim = -(-3 * width // 128) * 128
    padded = rows + EDGE
    npair = padded // 2
    opair = rows // 2
    tiles = lax.axis_size("tile")
    waves = lax.axis_size("wave")
    total_count = float(nimg * waves * rows * tiles * ncol)
    gsize = group_size(tiles)
    ngroup = tiles // gsize
    flipped = psf[:, ::-1].astype(F32)
    prow = jnp.concatenate(
        [flipped[:, HALO:], jnp.zeros((TAPS, ncol - TAPS), F32), flipped[:, :HALO]], axis=1
    )
    vmem = pl.BlockSpec(memory_space=pltpu.VMEM)
    smem = pl.BlockSpec(memory_space=pltpu.SMEM)
    dma = pltpu.SemaphoreType.DMA
    state, dual_out, misfit = pl.pallas_call(
        functools.partial(kernel, tiles, waves, total_count),
        out_shape=(
            jax.ShapeDtypeStruct((npar, rows, ncol), F32),
            jax.ShapeDtypeStruct((2, npar, rows, ncol), F32),
            jax.ShapeDtypeStruct((1,), F32),
        ),
        in_specs=[vmem] * 6 + [smem] * 4,
        out_specs=(vmem, vmem, smem),
        scratch_shapes=[
            pltpu.VMEM((PAIRS, 2 * ncol, 2 * ncol), BF16),
            pltpu.VMEM((nimg * rows, ncol), F32),
            pltpu.VMEM((images, padded, ncol), F32),
            pltpu.VMEM((width * padded, ncol), F32),
            pltpu.VMEM((npair * 2 * width, 2 * ncol), BF16),
            pltpu.VMEM((opair * 2 * width, 2 * ncol), BF16),
            pltpu.VMEM((npair * width, 2 * ncol), F32),
            pltpu.VMEM((npar, padded, ncol), F32),
            pltpu.VMEM((npar, rows + HALO, ncol), F32),
            pltpu.VMEM((npar, rows, ncol), F32),
            pltpu.VMEM((-(-npar // 8) * 8, nimg), F32),
            pltpu.VMEM((kdim, nimg), F32),
            pltpu.VMEM((nimg, kdim), BF16),
            pltpu.VMEM((2 * width, nimg), BF16),
            pltpu.VMEM((images, EDGE, ncol), BF16),
            pltpu.VMEM((images, EDGE, ncol), BF16),
            pltpu.VMEM((npar, HALO, ncol), F32),
            pltpu.VMEM((npar, HALO, ncol), F32),
            pltpu.VMEM((npar, HALO, ncol), F32),
            pltpu.VMEM((2, npar, padded, ncol), F32),
            pltpu.VMEM((2, waves, npar, padded, ncol), F32),
            pltpu.VMEM((2, npar, padded, ncol), F32),
            pltpu.VMEM((2, npar, EDGE, ncol), F32),
            pltpu.VMEM((2, npar, EDGE, ncol), F32),
            pltpu.VMEM((8, ncol), F32),
            pltpu.VMEM((waves, 8, ncol), F32),
            pltpu.VMEM((gsize, 8, ncol), F32),
            pltpu.VMEM((ngroup, 8, ncol), F32),
            dma((5,)), dma((5,)),
            dma((2, max(waves - 1, 1))), dma((2, max(waves - 1, 1))),
            dma((2, 2)), dma((2, 2)),
            dma((max(waves - 1, 1),)), dma((max(waves - 1, 1),)),
            dma((max(gsize - 1, 1),)), dma((max(gsize - 1, 1),)),
            dma((max(ngroup - 1, 1),)), dma((max(ngroup - 1, 1),)),
        ],
        compiler_params=pltpu.CompilerParams(
            collective_id=0, has_side_effects=True, vmem_limit_bytes=48 * 1024 * 1024
        ),
    )(
        params, dual_in, jacobian.reshape(images, rows, ncol),
        observed.reshape(nimg, rows, ncol), response, prow,
        step_size.reshape(1), dual_step.reshape(1), tv_bound.reshape(1), clip_bound.reshape(1),
    )
    return state, dual_out, misfit.reshape(())


def solution(mesh):
    in_specs = (
        P(None, "tile", None),
        P(None, None, "tile", None),
        P(None, None, "tile", None),
        P(None, "wave"),
        P(None, "wave", "tile", None),
        P(),
        P(),
        P(),
        P(),
        P(),
    )
    out_specs = (P(None, "tile", None), P(None, None, "tile", None), P())
    return jax.shard_map(
        per_device, mesh=mesh, in_specs=in_specs, out_specs=out_specs, check_vma=False
    )
```

time: 173 us -> 48.9 us (0.28); the launches traced: 171 us -> 48.5 us
  blocking collectives: 46.7 us -> 0 us
  Pallas kernels: 0 us -> 37.6 us
  matrix products: 28 us -> 0 us
  local copies, waits for them, and re-layouts: 31.2 us -> 5.71 us
  waiting for transfers between devices: 20.7 us -> 0 us
  starting transfers between devices: 20 us -> 0 us
  between operations: 19.2 us -> 5.1 us
  other arithmetic: 4.92 us -> 0.08 us
    pallas_call x0 -> x1, Pallas kernels: none -> 37.6 us  [per_device(): pl.pallas_call(functools.partial(kernel, tiles, waves, total_count), out_...]
    psum x1 -> x0, blocking collectives: 37 us -> none  [per_device(): misfit = lax.psum(huber, ('tile', 'wave')) / total_count]
    dot_general x73 -> x0, matrix products: 28 us -> none  [the longest x34 11.2 us: blur_rows(): jnp.einsum('nrk,jk->nrj', window, mats[16 - tap], preferred_element_type=...]
    unnamed x110 -> x12, local copies, waits for them, and re-layouts: 27.6 us -> 4.78 us
    ppermute x10 -> x0, starting transfers between devices: 19.9 us -> none  [the longest x4 18.5 us: padded_2(): lax.ppermute(lax.slice_in_dim(block, 0, width, axis=dim), axis, backward)]
    ppermute x10 -> x0, waiting for transfers between devices: 11.2 us -> none  [the longest x4 11.1 us: padded_2(): lax.ppermute(lax.slice_in_dim(block, block.shape[dim] - width, None, axis...]
    all_gather x2 -> x0, blocking collectives: 9.68 us -> none  [per_device(): state = lax.all_gather(state_share, 'wave', axis=1, tiled=True)]
    reduce_scatter x2 -> x0, waiting for transfers between devices: 9.54 us -> none  [per_device(): lax.psum_scatter(partial_grad, 'wave', scatter_dimension=1, tiled=True)]
  transfers between devices with their start and end apart: 12 -> 0, of which waited for: 4 -> 0; matrix products, arithmetic and copies ran while one was open for 21% -> 0% of each run, Pallas kernels for 0% -> 0%
where the time goes in v1:
time: 48.9 us; the launch traced here: 48.5 us
  Pallas kernels  37.6 us (77%)
  local copies, waits for them, and re-layouts  5.71 us (12%)
  between operations  5.1 us (10%)
    pallas_call x1, Pallas kernels, per_device(): pl.pallas_call(functools.partial(kernel, tiles, waves, total_count), out_...  37.6 us
    unnamed x12, local copies, waits for them, and re-layouts  4.78 us

profile of v1, /device:TPU:0, one launch (start us, length us, event | category | flops | bytes accessed | tf_op | source)
XLA Modules:
  0.0 48.5 jit_solution(6329720813438865996)
XLA Ops:
  0.6 0.0 copy-start.3
  3.3 0.1 pad.1.clone
  3.3 0.8 %rev.3 = bf16[17,17]{1,0:T(8,128)(2,1)S(1)} reverse(bf16[17,17]{1,0:T(8,128)(2,1)} %param.15), dimensions={1} | reverse | bytes 1156 | tf_op jit(solution)/shard_map/rev | solution.py:299
  4.1 0.1 slice.8
  4.2 0.0 copy-start.4
  4.2 0.1 pad_maximum_fusion.prow
  4.3 0.0 copy-done.3
  4.3 0.6 %copy-done.4 = f32[9,32]{1,0:T(8,128)S(1)} copy-done((f32[9,32]{1,0:T(8,128)S(1)}, f32[9,32]{1,0:T(8,128)}, u32[]{:S(2)}) %copy-start.4) | copy-done | bytes 1176
  4.9 0.0 copy-start
  4.9 1.0 %copy-done = bf16[4,32,16,128]{3,2,1,0:T(8,128)(2,1)S(1)} copy-done((bf16[4,32,16,128]{3,2,1,0:T(8,128)(2,1)S(1)}, bf16[4,32,16,128]{3,2,1,0:T(8,128)(2,1)}, u32[]{:S(2)}) %copy-start) | copy-done | bytes 524312
  5.9 0.0 copy-start.1
  5.9 0.9 %copy-done.1 = f32[2,9,16,128]{3,2,1,0:T(8,128)S(1)} copy-done((f32[2,9,16,128]{3,2,1,0:T(8,128)S(1)}, f32[2,9,16,128]{3,2,1,0:T(8,128)}, u32[]{:S(2)}) %copy-start.1) | copy-done | bytes 147480
  6.8 0.0 copy-start.2
  6.8 0.9 %copy-done.2 = bf16[4,9,16,128]{3,2,1,0:T(8,128)(2,1)S(1)} copy-done((bf16[4,9,16,128]{3,2,1,0:T(8,128)(2,1)S(1)}, bf16[4,9,16,128]{3,2,1,0:T(8,128)(2,1)}, u32[]{:S(2)}) %copy-start.2) | copy-done | bytes 147480
  7.8 37.6 %shard_map.121 = (f32[9,16,128]{2,1,0:T(8,128)S(1)}, f32[2,9,16,128]{3,2,1,0:T(8,128)S(1)}, f32[1]{0:T(128)}) custom-call(f32[9,16,128]{2,1,0:T(8,128)S(1)} %copy-done.3, f32[2,9,16,128]{3,2,1,0:T(8,128)S(1)} %copy-done.1, bf16[36,16,128]{2,1,0:T(8,128)(2,1)S(1)} %bitcast.12, bf16[128,16,128]{2,1,0:T(8,128)(2,1)S(1)} %bitcast.11, f32[9,32]{1,0:T(8,128)S(1)} %copy-done.4, ...), custom_call_target="tpu_custom_call" | custom-call | tf_op jit(solution)/shard_map/pallas_call | solution.py:306
  45.4 0.6 %copy.20 = f32[9,16,128]{2,1,0:T(8,128)} copy(f32[9,16,128]{2,1,0:T(8,128)S(1)} %get-tuple-element.12) | data formatting | bytes 147456
  46.0 0.7 %copy.21 = f32[2,9,16,128]{3,2,1,0:T(8,128)} copy(f32[2,9,16,128]{3,2,1,0:T(8,128)S(1)} %get-tuple-element.13) | data formatting | bytes 294912
  (2 shorter events, 0.0 us)
Async XLA Ops:
  0.6 3.6 %copy-start.3 = (f32[9,16,128]{2,1,0:T(8,128)S(1)}, f32[9,16,128]{2,1,0:T(8,128)}, u32[]{:S(2)}) copy-start(f32[9,16,128]{2,1,0:T(8,128)} %params.1) | copy-start | bytes 221188
  4.2 0.7 %copy-start.4 = (f32[9,32]{1,0:T(8,128)S(1)}, f32[9,32]{1,0:T(8,128)}, u32[]{:S(2)}) copy-start(f32[9,32]{1,0:T(8,128)} %response.1) | copy-start | bytes 3460
  4.9 1.0 %copy-start = (bf16[4,32,16,128]{3,2,1,0:T(8,128)(2,1)S(1)}, bf16[4,32,16,128]{3,2,1,0:T(8,128)(2,1)}, u32[]{:S(2)}) copy-start(bf16[4,32,16,128]{3,2,1,0:T(8,128)(2,1)} %param.14) | copy-start | bytes 1572868
  5.9 0.9 %copy-start.1 = (f32[2,9,16,128]{3,2,1,0:T(8,128)S(1)}, f32[2,9,16,128]{3,2,1,0:T(8,128)}, u32[]{:S(2)}) copy-start(f32[2,9,16,128]{3,2,1,0:T(8,128)} %dual.1) | copy-start | bytes 442372
  6.8 0.9 %copy-start.2 = (bf16[4,9,16,128]{3,2,1,0:T(8,128)(2,1)S(1)}, bf16[4,9,16,128]{3,2,1,0:T(8,128)(2,1)}, u32[]{:S(2)}) copy-start(bf16[4,9,16,128]{3,2,1,0:T(8,128)(2,1)} %param.12) | copy-start | bytes 442372

commit v2 on v1

v2 whole, which is shorter than its diff:
```python
import functools

import jax
import jax.numpy as jnp
from jax import lax
from jax.experimental import pallas as pl
from jax.experimental.pallas import tpu as pltpu
from jax.sharding import PartitionSpec as P

MESH = pl.DeviceIdType.MESH
HALO = 8
EDGE = 2 * HALO
TAPS = 17
PAIRS = 9
F32 = jnp.float32
BF16 = jnp.bfloat16


def split_hi_lo(value):
    high = value.astype(BF16).astype(F32)
    return high, value - high


def group_size(count):
    size = 1
    while size * size < count:
        size *= 2
    return size if count % size == 0 else count


def kernel(
    tiles, waves, total_count,
    params_h, dual_h, jac_h, obs_h, response, psf, step_size, dual_step, tv_bound, clip_bound,
    x_out, d_out, m_out,
    params, dual, jac, obs,
    mats, obs_f, jac_f, terms, pairs, proj, acc, xpad, dpad, base, respad, psfpad, rt, rbf, rtb,
    jac_edge, jac_up, jac_dn, par_up, par_dn, dual_up, div_edge, div_up, div_dn,
    full0, edge0, full1, edge1, full0_in, up0_in, dn0_in, full1_in, up1_in, dn1_in,
    m_own, m_mid, m_group, m_cross,
    local, in_send, in_recv, f_send, f_recv, u_send, u_recv, d_send, d_recv,
    mg_send, mg_recv, mc_send, mc_recv,
):
    npar, rows, ncol = params.shape
    images = jac.shape[0]
    stokes = images // npar
    nwave = response.shape[1]
    nimg = stokes * nwave
    width = -(-images // 8) * 8
    wide = -(-images // 16) * 16
    padded = rows + EDGE
    npair = padded // 2
    opair = rows // 2
    me_t = lax.axis_index("tile")
    me_w = lax.axis_index("wave")
    up = lax.rem(me_t + tiles - 1, tiles)
    down = lax.rem(me_t + 1, tiles)
    gsize = group_size(tiles)
    ngroup = tiles // gsize
    my_group = me_t // gsize
    my_place = lax.rem(me_t, gsize)
    spin = [me_w] + [lax.rem(me_w + d, waves) for d in range(1, waves)]
    group_tiles = [me_t]
    group_tiles += [my_group * gsize + lax.rem(my_place + d, gsize) for d in range(1, gsize)]
    group_peers = [(t, w) for i, t in enumerate(group_tiles) for j, w in enumerate(spin) if i + j > 0]
    cross_peers = [
        (lax.rem(my_group + d, ngroup) * gsize + my_place, me_w) for d in range(1, ngroup)
    ]

    barrier = pltpu.get_barrier_semaphore()
    peers = [(t, w) for w in spin for t in (up, down)] + group_peers + cross_peers
    for peer in peers:
        pl.semaphore_signal(barrier, inc=1, device_id=peer, device_id_type=MESH)
    fetch = [
        pltpu.make_async_copy(jac_h, jac, local.at[0]),
        pltpu.make_async_copy(params_h, params, local.at[1]),
        pltpu.make_async_copy(dual_h, dual, local.at[2]),
        pltpu.make_async_copy(obs_h, obs, local.at[3]),
    ]
    for copy in fetch:
        copy.start()
    fetch[0].wait()
    for m in range(images):
        jac_f[m, HALO:HALO + rows, :] = jac[m].astype(F32)
    jac_edge[0] = jac_f[:, HALO:EDGE, :].reshape(images * HALO, ncol).astype(BF16)
    jac_edge[1] = jac_f[:, rows:rows + HALO, :].reshape(images * HALO, ncol).astype(BF16)
    fetch[1].wait()
    fetch[2].wait()
    pl.semaphore_wait(barrier, len(peers))

    def remote(src, dst, send, recv, peer):
        return pltpu.make_async_remote_copy(
            src_ref=src, dst_ref=dst, send_sem=send, recv_sem=recv,
            device_id=peer, device_id_type=MESH,
        )

    above, below = (up, me_w), (down, me_w)
    first = [
        remote(params.at[:, pl.ds(rows - HALO, HALO)], par_up, in_send.at[0], in_recv.at[0], below),
        remote(params.at[:, pl.ds(0, HALO)], par_dn, in_send.at[1], in_recv.at[1], above),
        remote(dual.at[0, :, pl.ds(rows - HALO, HALO)], dual_up, in_send.at[2], in_recv.at[2], below),
        remote(jac_edge.at[1], jac_up, in_send.at[3], in_recv.at[3], below),
        remote(jac_edge.at[0], jac_dn, in_send.at[4], in_recv.at[4], above),
    ]
    for copy in first:
        copy.start()

    step = step_size[0]
    clip = clip_bound[0]
    bound = tv_bound[0]
    dstep = dual_step[0]

    zero_block = jnp.zeros((ncol, ncol), BF16)
    mats[0, ncol:, 0:ncol] = zero_block
    mats[PAIRS - 1, 0:ncol, ncol:] = zero_block
    psfpad[...] = jnp.zeros_like(psfpad)
    psfpad[0:TAPS, 0:TAPS] = psf[...].astype(F32)
    taps = pltpu.roll(psfpad[...], ncol - HALO, 1)
    for tap in range(TAPS):
        line = jnp.broadcast_to(taps[tap:tap + 1, :], (ncol, ncol))
        block = pltpu.roll(line, 0, 1, stride=1, stride_axis=0).astype(BF16)
        if tap % 2 == 0:
            mats[tap // 2, 0:ncol, 0:ncol] = block
            mats[tap // 2, ncol:, ncol:] = block
        else:
            mats[tap // 2, 0:ncol, ncol:] = block
            mats[tap // 2 + 1, ncol:, 0:ncol] = block

    respad[...] = jnp.zeros_like(respad)
    respad[0:npar, 0:nwave] = response[...]
    rt[...] = jnp.zeros_like(rt)
    spread = respad[...]
    for s in range(stokes):
        shifted = spread if s == 0 else pltpu.roll(spread, s * nwave, 1)
        for part in range(3):
            at = part * width + s * npar
            rt[at:at + npar, :] = shifted[0:npar]
    full = rt[...]
    high, low = split_hi_lo(full)
    place = lax.broadcasted_iota(jnp.int32, full.shape, 0)
    rbf[...] = jnp.where(place < 2 * width, high, low).T.astype(BF16)
    rtb[...] = jnp.concatenate([high[0:width], low[0:width]], axis=0).astype(BF16)

    for m in range(images, width):
        terms[m * padded:(m + 1) * padded, :] = jnp.zeros((padded, ncol), F32)
    d1 = params[...]
    xpad[:, HALO:HALO + rows, :] = d1
    d1 = pltpu.roll(d1, ncol - 1, 2) - d1
    d1 = jnp.clip(dual[1] + dstep * d1, -bound, bound)
    d_out[1] = d1
    fetch[3].wait()
    obs_f[...] = obs[...].astype(F32).reshape(nimg * rows, ncol)

    for copy in first:
        copy.wait()
    xpad[:, 0:HALO, :] = par_up[...]
    xpad[:, HALO + rows:, :] = par_dn[...]
    d0 = xpad[:, HALO + 1:HALO + 1 + rows, :] - xpad[:, HALO:HALO + rows, :]
    d0 = jnp.clip(dual[0] + dstep * d0, -bound, bound)
    d_out[0] = d0
    side = xpad[:, 1:HALO + 1, :] - xpad[:, 0:HALO, :]
    dpad[:, 0:HALO, :] = jnp.clip(dual_up[...] + dstep * side, -bound, bound)
    dpad[:, HALO:, :] = d0
    div = (d0 - dpad[:, HALO - 1:HALO - 1 + rows, :]) + (d1 - pltpu.roll(d1, 1, 2))
    base[:, HALO:HALO + rows, :] = div
    div_edge[0] = div[:, 0:HALO, :]
    div_edge[1] = div[:, rows - HALO:, :]
    copies_v = [
        remote(div_edge.at[1], div_up, in_send.at[5], in_recv.at[5], below),
        remote(div_edge.at[0], div_dn, in_send.at[6], in_recv.at[6], above),
    ]
    for copy in copies_v:
        copy.start()
    jac_f[:, 0:HALO, :] = jac_up[...].astype(F32).reshape(images, HALO, ncol)
    jac_f[:, HALO + rows:, :] = jac_dn[...].astype(F32).reshape(images, HALO, ncol)

    zero_k = jnp.zeros((rbf.shape[1] - 3 * width, 2 * ncol), F32)

    def widen(value):
        if wide == width:
            return value.astype(BF16)
        fill = jnp.zeros((wide - width, value.shape[1]), F32)
        return jnp.concatenate([value, fill], axis=0).astype(BF16)

    for it in range(2):
        for m in range(images):
            terms[m * padded:(m + 1) * padded, :] = jac_f[m] * xpad[m % npar]
        for q in range(npair):
            for i in range(2):
                value = terms[pl.ds(2 * q + i, width, stride=padded), :]
                pairs[q * wide:(q + 1) * wide, i * ncol:(i + 1) * ncol] = widen(value)
        total = None
        for k in range(PAIRS):
            window = pairs[k * wide:(k + opair) * wide, :]
            part = lax.dot_general(
                window, mats[k], (((1,), (1,)), ((), ())), preferred_element_type=F32
            )
            total = part if total is None else total + part
        loss = jnp.zeros((8, ncol), F32)
        for r in range(opair):
            bhi, blo = split_hi_lo(total[r * wide:r * wide + width])
            stack = jnp.concatenate([bhi, blo, bhi, zero_k], axis=0).astype(BF16)
            blurred = jnp.dot(rbf[...], stack, preferred_element_type=F32)
            halves = []
            for i in range(2):
                target = obs_f[pl.ds(2 * r + i, nimg, stride=rows), :]
                resid = blurred[:, i * ncol:(i + 1) * ncol] - target
                held = jnp.clip(resid, -clip, clip)
                if it == 0:
                    huber = held * (resid - 0.5 * held)
                    loss = loss + jnp.sum(huber.reshape(nimg // 8, 8, ncol), axis=0)
                halves.append(held.astype(BF16))
            weighted = jnp.concatenate(halves, axis=1)
            both = jnp.dot(rtb[...], weighted, preferred_element_type=F32)
            proj[r * wide:(r + 1) * wide, :] = widen(both[:width] + both[width:])
        if it == 0:
            m_own[...] = loss
            slot = my_place * waves + me_w
            m_group[slot] = loss
            copies_g = [
                remote(m_own, m_group.at[slot], mg_send.at[d], mg_recv.at[d], peer)
                for d, peer in enumerate(group_peers)
            ]
            for copy in copies_g:
                copy.start()
        for k in range(PAIRS):
            back = jnp.dot(proj[...], mats[k], preferred_element_type=F32)
            for q in range(opair):
                part = back[q * wide:(q + 1) * wide]
                at = (k + q) * wide
                if k == 0 or q == opair - 1:
                    acc[at:at + wide, :] = part
                else:
                    acc[at:at + wide, :] += part
        for q in range(npair):
            for i in range(2):
                value = acc[q * wide:q * wide + width, i * ncol:(i + 1) * ncol]
                terms[pl.ds(2 * q + i, width, stride=padded), :] = value
        grads = []
        for p in range(npar):
            grad = None
            for s in range(stokes):
                m = s * npar + p
                part = jac_f[m] * terms[m * padded:(m + 1) * padded, :]
                grad = part if grad is None else grad + part
            grads.append(grad)
        reach = EDGE if it == 0 else HALO
        whole = grads if it == 0 else [g[HALO:HALO + rows] for g in grads]
        whole = jnp.concatenate(whole, axis=0).astype(BF16)
        full_out, edge_out = (full0, edge0) if it == 0 else (full1, edge1)
        full_in, up_in, dn_in = (full0_in, up0_in, dn0_in) if it == 0 else (full1_in, up1_in, dn1_in)
        edge_out[0] = jnp.concatenate([g[:reach] for g in grads], axis=0).astype(BF16)
        edge_out[1] = jnp.concatenate([g[padded - reach:] for g in grads], axis=0).astype(BF16)
        full_out[...] = whole
        full_in[me_w] = whole
        copies = []
        for d in range(waves - 1, -1, -1):
            copies += [
                remote(edge_out.at[1], up_in.at[me_w], u_send.at[it, d], u_recv.at[it, d], (down, spin[d])),
                remote(edge_out.at[0], dn_in.at[me_w], d_send.at[it, d], d_recv.at[it, d], (up, spin[d])),
            ]
        for d in range(1, waves):
            copies.append(
                remote(full_out, full_in.at[me_w], f_send.at[it, d], f_recv.at[it, d], (me_t, spin[d]))
            )
        for copy in copies:
            copy.start()
        if it == 0:
            for copy in copies_v:
                copy.wait()
            base[:, 0:HALO, :] = div_up[...]
            base[:, HALO + rows:, :] = div_dn[...]
            base[...] = xpad[...] + step * base[...]
        for copy in copies:
            copy.wait()

        def added(ref, count):
            value = ref[0].astype(F32)
            for w in range(1, waves):
                value = value + ref[w].astype(F32)
            return value.reshape(npar, count, ncol)

        span = padded if it == 0 else rows
        inner = added(full_in, span)
        top = inner[:, :reach] + added(up_in, reach)
        low = inner[:, span - reach:] + added(dn_in, reach)
        if it == 0:
            kept = [base[:, :reach, :] - step * top]
            if span > 2 * reach:
                kept.append(base[:, reach:span - reach, :] - step * inner[:, reach:span - reach])
            kept.append(base[:, span - reach:, :] - step * low)
            mid = base[:, HALO:HALO + rows, :] - xpad[:, HALO:HALO + rows, :]
            at = 0
            for value in kept:
                xpad[:, at:at + value.shape[1], :] = value
                at += value.shape[1]
            base[:, HALO:HALO + rows, :] = xpad[:, HALO:HALO + rows, :] + mid
            for copy in copies_g:
                copy.wait()
            total_m = m_group[0]
            for g in range(1, gsize * waves):
                total_m = total_m + m_group[g]
            m_mid[...] = total_m
            m_cross[my_group] = total_m
            copies_c = [
                remote(m_mid, m_cross.at[my_group], mc_send.at[d], mc_recv.at[d], peer)
                for d, peer in enumerate(cross_peers)
            ]
            for copy in copies_c:
                copy.start()
        else:
            x_out[:, 0:reach, :] = base[:, HALO:HALO + reach, :] - step * top
            if span > 2 * reach:
                x_out[:, reach:span - reach, :] = (
                    base[:, HALO + reach:HALO + span - reach, :] - step * inner[:, reach:span - reach]
                )
            x_out[:, span - reach:, :] = base[:, HALO + span - reach:HALO + span, :] - step * low
            for copy in copies_c:
                copy.wait()
            tot = m_cross[0]
            for g in range(1, ngroup):
                tot = tot + m_cross[g]
            m_out[0] = jnp.sum(tot) / total_count


def per_device(
    params, dual_in, jacobian, response, observed, psf, step_size, dual_step, tv_bound, clip_bound
):
    stokes, nwave, rows, ncol = observed.shape
    npar = params.shape[0]
    nimg = stokes * nwave
    images = stokes * npar
    width = -(-images // 8) * 8
    wide = -(-images // 16) * 16
    kdim = -(-3 * width // 128) * 128
    padded = rows + EDGE
    npair = padded // 2
    opair = rows // 2
    tiles = lax.axis_size("tile")
    waves = lax.axis_size("wave")
    total_count = float(nimg * waves * rows * tiles * ncol)
    gsize = group_size(tiles)
    ngroup = tiles // gsize
    vmem = pl.BlockSpec(memory_space=pltpu.VMEM)
    smem = pl.BlockSpec(memory_space=pltpu.SMEM)
    hbm = pl.BlockSpec(memory_space=pltpu.HBM)
    dma = pltpu.SemaphoreType.DMA
    state, dual_out, misfit = pl.pallas_call(
        functools.partial(kernel, tiles, waves, total_count),
        out_shape=(
            jax.ShapeDtypeStruct((npar, rows, ncol), F32),
            jax.ShapeDtypeStruct((2, npar, rows, ncol), F32),
            jax.ShapeDtypeStruct((1,), F32),
        ),
        in_specs=[hbm] * 4 + [vmem] * 2 + [smem] * 4,
        out_specs=(vmem, vmem, smem),
        scratch_shapes=[
            pltpu.VMEM((npar, rows, ncol), F32),
            pltpu.VMEM((2, npar, rows, ncol), F32),
            pltpu.VMEM((images, rows, ncol), BF16),
            pltpu.VMEM((nimg, rows, ncol), BF16),
            pltpu.VMEM((PAIRS, 2 * ncol, 2 * ncol), BF16),
            pltpu.VMEM((nimg * rows, ncol), F32),
            pltpu.VMEM((images, padded, ncol), F32),
            pltpu.VMEM((width * padded, ncol), F32),
            pltpu.VMEM((npair * wide, 2 * ncol), BF16),
            pltpu.VMEM((opair * wide, 2 * ncol), BF16),
            pltpu.VMEM((npair * wide, 2 * ncol), F32),
            pltpu.VMEM((npar, padded, ncol), F32),
            pltpu.VMEM((npar, rows + HALO, ncol), F32),
            pltpu.VMEM((npar, padded, ncol), F32),
            pltpu.VMEM((-(-npar // 8) * 8, nimg), F32),
            pltpu.VMEM((-(-TAPS // 8) * 8, ncol), F32),
            pltpu.VMEM((kdim, nimg), F32),
            pltpu.VMEM((nimg, kdim), BF16),
            pltpu.VMEM((2 * width, nimg), BF16),
            pltpu.VMEM((2, images * HALO, ncol), BF16),
            pltpu.VMEM((images * HALO, ncol), BF16),
            pltpu.VMEM((images * HALO, ncol), BF16),
            pltpu.VMEM((npar, HALO, ncol), F32),
            pltpu.VMEM((npar, HALO, ncol), F32),
            pltpu.VMEM((npar, HALO, ncol), F32),
            pltpu.VMEM((2, npar, HALO, ncol), F32),
            pltpu.VMEM((npar, HALO, ncol), F32),
            pltpu.VMEM((npar, HALO, ncol), F32),
            pltpu.VMEM((npar * padded, ncol), BF16),
            pltpu.VMEM((2, npar * EDGE, ncol), BF16),
            pltpu.VMEM((npar * rows, ncol), BF16),
            pltpu.VMEM((2, npar * HALO, ncol), BF16),
            pltpu.VMEM((waves, npar * padded, ncol), BF16),
            pltpu.VMEM((waves, npar * EDGE, ncol), BF16),
            pltpu.VMEM((waves, npar * EDGE, ncol), BF16),
            pltpu.VMEM((waves, npar * rows, ncol), BF16),
            pltpu.VMEM((waves, npar * HALO, ncol), BF16),
            pltpu.VMEM((waves, npar * HALO, ncol), BF16),
            pltpu.VMEM((8, ncol), F32),
            pltpu.VMEM((8, ncol), F32),
            pltpu.VMEM((gsize * waves, 8, ncol), F32),
            pltpu.VMEM((ngroup, 8, ncol), F32),
            dma((4,)),
            dma((7,)), dma((7,)),
            dma((2, waves)), dma((2, waves)),
            dma((2, waves)), dma((2, waves)),
            dma((2, waves)), dma((2, waves)),
            dma((gsize * waves,)), dma((gsize * waves,)),
            dma((ngroup,)), dma((ngroup,)),
        ],
        compiler_params=pltpu.CompilerParams(
            collective_id=0, has_side_effects=True, vmem_limit_bytes=48 * 1024 * 1024
        ),
    )(
        params, dual_in, jacobian.reshape(images, rows, ncol),
        observed.reshape(nimg, rows, ncol), response, psf,
        step_size.reshape(1), dual_step.reshape(1), tv_bound.reshape(1), clip_bound.reshape(1),
    )
    return state, dual_out, misfit.reshape(())


def solution(mesh):
    in_specs = (
        P(None, "tile", None),
        P(None, None, "tile", None),
        P(None, None, "tile", None),
        P(None, "wave"),
        P(None, "wave", "tile", None),
        P(),
        P(),
        P(),
        P(),
        P(),
    )
    out_specs = (P(None, "tile", None), P(None, None, "tile", None), P())
    return jax.shard_map(
        per_device, mesh=mesh, in_specs=in_specs, out_specs=out_specs, check_vma=False
    )
```

time: 48.9 us -> 38 us (0.78)
  Pallas kernels: 37.6 us -> 27.6 us
  local copies, waits for them, and re-layouts: 5.71 us -> 5.04 us
    pallas_call x1, Pallas kernels: 37.6 us -> 27.6 us  [per_device(): pl.pallas_call(functools.partial(kernel, tiles, waves, total_count), out_...]
    rev x1 -> x0, local copies, waits for them, and re-layouts: 0.77 us -> none  [per_device(): flipped = psf[:, ::-1].astype(F32)]
    unnamed x12 -> x14, local copies, waits for them, and re-layouts: 4.78 us -> 5.04 us
where the time goes in v2:
time: 38 us; the launch traced here: 37.6 us
  Pallas kernels  27.6 us (73%)
  local copies, waits for them, and re-layouts  5.04 us (13%)
  between operations  4.98 us (13%)
    pallas_call x1, Pallas kernels, per_device(): pl.pallas_call(functools.partial(kernel, tiles, waves, total_count), out_...  27.6 us
    unnamed x14, local copies, waits for them, and re-layouts  5.04 us

profile of v2, /device:TPU:0, one launch (start us, length us, event | category | flops | bytes accessed | tf_op | source)
XLA Modules:
  0.0 37.6 jit_solution(3102629612539386257)
XLA Ops:
  1.3 0.0 copy-start.4
  1.9 0.0 copy-start.5
  3.3 0.0 copy-done.4
  3.3 0.0 copy-done.5
  3.3 0.0 copy-start
  3.3 1.0 %copy-done = bf16[4,32,16,128]{3,2,1,0:T(8,128)(2,1)S(1)} copy-done((bf16[4,32,16,128]{3,2,1,0:T(8,128)(2,1)S(1)}, bf16[4,32,16,128]{3,2,1,0:T(8,128)(2,1)}, u32[]{:S(2)}) %copy-start) | copy-done | bytes 524312
  4.3 0.0 copy-start.1
  4.3 0.9 %copy-done.1 = f32[2,9,16,128]{3,2,1,0:T(8,128)S(1)} copy-done((f32[2,9,16,128]{3,2,1,0:T(8,128)S(1)}, f32[2,9,16,128]{3,2,1,0:T(8,128)}, u32[]{:S(2)}) %copy-start.1) | copy-done | bytes 147480
  5.2 0.0 copy-start.2
  5.2 0.9 %copy-done.2 = bf16[4,9,16,128]{3,2,1,0:T(8,128)(2,1)S(1)} copy-done((bf16[4,9,16,128]{3,2,1,0:T(8,128)(2,1)S(1)}, bf16[4,9,16,128]{3,2,1,0:T(8,128)(2,1)}, u32[]{:S(2)}) %copy-start.2) | copy-done | bytes 147480
  6.1 0.0 copy-start.3
  6.1 0.9 %copy-done.3 = f32[9,16,128]{2,1,0:T(8,128)S(1)} copy-done((f32[9,16,128]{2,1,0:T(8,128)S(1)}, f32[9,16,128]{2,1,0:T(8,128)}, u32[]{:S(2)}) %copy-start.3) | copy-done | bytes 73752
  7.0 27.6 %shard_map.121 = (f32[9,16,128]{2,1,0:T(8,128)S(1)}, f32[2,9,16,128]{3,2,1,0:T(8,128)S(1)}, f32[1]{0:T(128)}) custom-call(f32[9,16,128]{2,1,0:T(8,128)S(1)} %copy-done.3, f32[2,9,16,128]{3,2,1,0:T(8,128)S(1)} %copy-done.1, bf16[36,16,128]{2,1,0:T(8,128)(2,1)S(1)} %bitcast.12, bf16[128,16,128]{2,1,0:T(8,128)(2,1)S(1)} %bitcast.11, f32[9,32]{1,0:T(8,128)S(1)} %copy-done.4, ...), custom_call_target="tpu_custom_call" | custom-call | tf_op jit(solution)/shard_map/pallas_call | solution.py:347
  34.7 0.6 %copy.20 = f32[9,16,128]{2,1,0:T(8,128)} copy(f32[9,16,128]{2,1,0:T(8,128)S(1)} %get-tuple-element.12) | data formatting | bytes 147456
  35.3 0.7 %copy.21 = f32[2,9,16,128]{3,2,1,0:T(8,128)} copy(f32[2,9,16,128]{3,2,1,0:T(8,128)S(1)} %get-tuple-element.13) | data formatting | bytes 294912
Async XLA Ops:
  1.3 2.0 %copy-start.4 = (f32[9,32]{1,0:T(8,128)S(1)}, f32[9,32]{1,0:T(8,128)}, u32[]{:S(2)}) copy-start(f32[9,32]{1,0:T(8,128)} %response.1) | copy-start | bytes 3460
  1.9 1.3 %copy-start.5 = (bf16[17,17]{1,0:T(8,128)(2,1)S(1)}, bf16[17,17]{1,0:T(8,128)(2,1)}, u32[]{:S(2)}) copy-start(bf16[17,17]{1,0:T(8,128)(2,1)} %psf.1) | copy-start | bytes 1738
  3.3 1.0 %copy-start = (bf16[4,32,16,128]{3,2,1,0:T(8,128)(2,1)S(1)}, bf16[4,32,16,128]{3,2,1,0:T(8,128)(2,1)}, u32[]{:S(2)}) copy-start(bf16[4,32,16,128]{3,2,1,0:T(8,128)(2,1)} %param.14) | copy-start | bytes 1572868
  4.3 0.9 %copy-start.1 = (f32[2,9,16,128]{3,2,1,0:T(8,128)S(1)}, f32[2,9,16,128]{3,2,1,0:T(8,128)}, u32[]{:S(2)}) copy-start(f32[2,9,16,128]{3,2,1,0:T(8,128)} %dual_h.1) | copy-start | bytes 442372
  5.2 0.9 %copy-start.2 = (bf16[4,9,16,128]{3,2,1,0:T(8,128)(2,1)S(1)}, bf16[4,9,16,128]{3,2,1,0:T(8,128)(2,1)}, u32[]{:S(2)}) copy-start(bf16[4,9,16,128]{3,2,1,0:T(8,128)(2,1)} %param.12) | copy-start | bytes 442372
  6.1 0.9 %copy-start.3 = (f32[9,16,128]{2,1,0:T(8,128)S(1)}, f32[9,16,128]{2,1,0:T(8,128)}, u32[]{:S(2)}) copy-start(f32[9,16,128]{2,1,0:T(8,128)} %params_h.1) | copy-start | bytes 221188

commit v3 on v2

--- a/solution.py
+++ b/solution.py
@@ -187,17 +187,19 @@
         for q in range(npair):
             for i in range(2):
                 value = terms[pl.ds(2 * q + i, width, stride=padded), :]
-                pairs[q * wide:(q + 1) * wide, i * ncol:(i + 1) * ncol] = widen(value)
+                value = jnp.concatenate(split_hi_lo(value), axis=0).astype(BF16)
+                pairs[q * 2 * width:(q + 1) * 2 * width, i * ncol:(i + 1) * ncol] = value
         total = None
         for k in range(PAIRS):
-            window = pairs[k * wide:(k + opair) * wide, :]
+            window = pairs[k * 2 * width:(k + opair) * 2 * width, :]
             part = lax.dot_general(
                 window, mats[k], (((1,), (1,)), ((), ())), preferred_element_type=F32
             )
             total = part if total is None else total + part
         loss = jnp.zeros((8, ncol), F32)
         for r in range(opair):
-            bhi, blo = split_hi_lo(total[r * wide:r * wide + width])
+            both = total[r * 2 * width:(r + 1) * 2 * width]
+            bhi, blo = split_hi_lo(both[:width] + both[width:])
             stack = jnp.concatenate([bhi, blo, bhi, zero_k], axis=0).astype(BF16)
             blurred = jnp.dot(rbf[...], stack, preferred_element_type=F32)
             halves = []
@@ -362,7 +364,7 @@
             pltpu.VMEM((nimg * rows, ncol), F32),
             pltpu.VMEM((images, padded, ncol), F32),
             pltpu.VMEM((width * padded, ncol), F32),
-            pltpu.VMEM((npair * wide, 2 * ncol), BF16),
+            pltpu.VMEM((npair * 2 * width, 2 * ncol), BF16),
             pltpu.VMEM((opair * wide, 2 * ncol), BF16),
             pltpu.VMEM((npair * wide, 2 * ncol), F32),
             pltpu.VMEM((npar, padded, ncol), F32),
@@ -405,7 +407,7 @@
             dma((ngroup,)), dma((ngroup,)),
         ],
         compiler_params=pltpu.CompilerParams(
-            collective_id=0, has_side_effects=True, vmem_limit_bytes=48 * 1024 * 1024
+            collective_id=0, has_side_effects=True, vmem_limit_bytes=66_000_000
         ),
     )(
         params, dual_in, jacobian.reshape(images, rows, ncol),

time: 38 us -> 37.4 us (0.984)
  local copies, waits for them, and re-layouts: 5.04 us -> 2.22 us
  Pallas kernels: 27.6 us -> 29.9 us
    unnamed x14 -> x4, local copies, waits for them, and re-layouts: 5.04 us -> 2.22 us
    pallas_call x1, Pallas kernels: 27.6 us -> 29.9 us  [per_device(): pl.pallas_call(functools.partial(kernel, tiles, waves, total_count), out_...]
where the time goes in v3:
time: 37.4 us; the launch traced here: 37.1 us
  Pallas kernels  29.9 us (80%)
  between operations  5 us (13%)
  local copies, waits for them, and re-layouts  2.22 us (6%)
    pallas_call x1, Pallas kernels, per_device(): pl.pallas_call(functools.partial(kernel, tiles, waves, total_count), out_...  29.9 us
    unnamed x4, local copies, waits for them, and re-layouts  2.22 us

profile of v3, /device:TPU:0, one launch (start us, length us, event | category | flops | bytes accessed | tf_op | source)
XLA Modules:
  0.0 37.1 jit_solution(14583184764881475004)
XLA Ops:
  3.2 29.9 %shard_map.121 = (f32[9,16,128]{2,1,0:T(8,128)}, f32[2,9,16,128]{3,2,1,0:T(8,128)}, f32[1]{0:T(128)}) custom-call(f32[9,16,128]{2,1,0:T(8,128)} %params_h.1, f32[2,9,16,128]{3,2,1,0:T(8,128)} %dual_h.1, bf16[36,16,128]{2,1,0:T(8,128)(2,1)} %bitcast.12, bf16[128,16,128]{2,1,0:T(8,128)(2,1)} %bitcast.11, f32[9,32]{1,0:T(8,128)} %response.1, ...), custom_call_target="tpu_custom_call" | custom-call | tf_op jit(solution)/shard_map/pallas_call | solution.py:349
  33.1 0.0 copy-start
  33.1 1.6 %copy.20 = f32[9,16,128]{2,1,0:T(8,128)} copy(f32[9,16,128]{2,1,0:T(8,128)} %get-tuple-element.12) | data formatting | bytes 147456
  34.6 0.0 copy-done
  34.6 0.7 %copy.21 = f32[2,9,16,128]{3,2,1,0:T(8,128)} copy(f32[2,9,16,128]{3,2,1,0:T(8,128)S(1)} %copy-done) | data formatting | bytes 294912
Async XLA Ops:
  33.1 1.6 %copy-start = (f32[2,9,16,128]{3,2,1,0:T(8,128)S(1)}, f32[2,9,16,128]{3,2,1,0:T(8,128)}, u32[]{:S(2)}) copy-start(f32[2,9,16,128]{3,2,1,0:T(8,128)} %get-tuple-element.13) | copy-start | bytes 442372

commit v4 on v3

--- a/solution.py
+++ b/solution.py
@@ -31,8 +31,8 @@
 def kernel(
     tiles, waves, total_count,
     params_h, dual_h, jac_h, obs_h, response, psf, step_size, dual_step, tv_bound, clip_bound,
-    x_out, d_out, m_out,
-    params, dual, jac, obs,
+    x_out, d_out_h, m_out,
+    d_out, params, dual, jac, obs,
     mats, obs_f, jac_f, terms, pairs, proj, acc, xpad, dpad, base, respad, psfpad, rt, rbf, rtb,
     jac_edge, jac_up, jac_dn, par_up, par_dn, dual_up, div_edge, div_up, div_dn,
     full0, edge0, full1, edge1, full0_in, up0_in, dn0_in, full1_in, up1_in, dn1_in,
@@ -173,6 +173,8 @@
     jac_f[:, 0:HALO, :] = jac_up[...].astype(F32).reshape(images, HALO, ncol)
     jac_f[:, HALO + rows:, :] = jac_dn[...].astype(F32).reshape(images, HALO, ncol)
 
+    keep = pltpu.make_async_copy(d_out, d_out_h, local.at[4])
+    keep.start()
     zero_k = jnp.zeros((rbf.shape[1] - 3 * width, 2 * ncol), F32)
 
     def widen(value):
@@ -316,7 +318,7 @@
                     base[:, HALO + reach:HALO + span - reach, :] - step * inner[:, reach:span - reach]
                 )
             x_out[:, span - reach:, :] = base[:, HALO + span - reach:HALO + span, :] - step * low
-            for copy in copies_c:
+            for copy in copies_c + [keep]:
                 copy.wait()
             tot = m_cross[0]
             for g in range(1, ngroup):
@@ -354,8 +356,9 @@
             jax.ShapeDtypeStruct((1,), F32),
         ),
         in_specs=[hbm] * 4 + [vmem] * 2 + [smem] * 4,
-        out_specs=(vmem, vmem, smem),
+        out_specs=(vmem, hbm, smem),
         scratch_shapes=[
+            pltpu.VMEM((2, npar, rows, ncol), F32),
             pltpu.VMEM((npar, rows, ncol), F32),
             pltpu.VMEM((2, npar, rows, ncol), F32),
             pltpu.VMEM((images, rows, ncol), BF16),
@@ -398,7 +401,7 @@
             pltpu.VMEM((8, ncol), F32),
             pltpu.VMEM((gsize * waves, 8, ncol), F32),
             pltpu.VMEM((ngroup, 8, ncol), F32),
-            dma((4,)),
+            dma((5,)),
             dma((7,)), dma((7,)),
             dma((2, waves)), dma((2, waves)),
             dma((2, waves)), dma((2, waves)),

time: 37.4 us -> 37.3 us (level)
  no operation moved by 1% of the time
where the time goes in v4:
time: 37.3 us; the launch traced here: 37 us
  Pallas kernels  29.8 us (80%)
  between operations  5 us (13%)
  local copies, waits for them, and re-layouts  2.22 us (6%)
    pallas_call x1, Pallas kernels, per_device(): pl.pallas_call(functools.partial(kernel, tiles, waves, total_count), out_...  29.8 us
    unnamed x4, local copies, waits for them, and re-layouts  2.22 us

profile of v4, /device:TPU:0, one launch (start us, length us, event | category | flops | bytes accessed | tf_op | source)
XLA Modules:
  0.0 37.0 jit_solution(14840823134174469831)
XLA Ops:
  3.2 29.8 %shard_map.121 = (f32[9,16,128]{2,1,0:T(8,128)}, f32[2,9,16,128]{3,2,1,0:T(8,128)}, f32[1]{0:T(128)}) custom-call(f32[9,16,128]{2,1,0:T(8,128)} %params_h.1, f32[2,9,16,128]{3,2,1,0:T(8,128)} %dual_h.1, bf16[36,16,128]{2,1,0:T(8,128)(2,1)} %bitcast.12, bf16[128,16,128]{2,1,0:T(8,128)(2,1)} %bitcast.11, f32[9,32]{1,0:T(8,128)} %response.1, ...), custom_call_target="tpu_custom_call" | custom-call | tf_op jit(solution)/shard_map/pallas_call | solution.py:351
  33.0 0.0 copy-start
  33.0 1.6 %copy.20 = f32[9,16,128]{2,1,0:T(8,128)} copy(f32[9,16,128]{2,1,0:T(8,128)} %get-tuple-element.12) | data formatting | bytes 147456
  34.6 0.0 copy-done
  34.6 0.7 %copy.21 = f32[2,9,16,128]{3,2,1,0:T(8,128)} copy(f32[2,9,16,128]{3,2,1,0:T(8,128)S(1)} %copy-done) | data formatting | bytes 294912
Async XLA Ops:
  33.0 1.6 %copy-start = (f32[2,9,16,128]{3,2,1,0:T(8,128)S(1)}, f32[2,9,16,128]{3,2,1,0:T(8,128)}, u32[]{:S(2)}) copy-start(f32[2,9,16,128]{3,2,1,0:T(8,128)} %get-tuple-element.13) | copy-start | bytes 442372
